TPU v7x, 256 devices: a whole 4x4x8 slice. The times are simulated.
256 devices in a mesh: req: 32 (over z, y), tp: 8 (over x, core).
Axes of the slice: x: 4, y: 4, z: 8, core: 2. Of those that a mesh axis runs over, the one named last changes fastest.
Arguments:
- hidden: bfloat16 [9472, 5120], P('req', 'tp'), may hold values from -6 to 6
- raw_q: bfloat16 [9472, 3072], P('req', 'tp'), may hold values from -70 to 70
- raw_k: bfloat16 [9472, 3072], P('req', 'tp'), may hold values from -70 to 70
- raw_v: bfloat16 [9472, 3072], P('req', 'tp'), may hold values from -6 to 6
- q_gain: float32 [3072], P('tp'), may hold values from 0.5 to 2
- k_gain: float32 [3072], P('tp'), may hold values from 0.5 to 2
- out_weight: bfloat16 [3072, 5120], P('tp'), may hold values from -0.109375 to 0.109375
- post_gain: float32 [5120], P('tp'), may hold values from 0.25 to 1.75
- prefix_keys: bfloat16 [32, 32, 128, 3072], P(None, 'req', None, 'tp'), may hold values from -420 to 420
- prefix_values: bfloat16 [32, 32, 128, 3072], P(None, 'req', None, 'tp'), may hold values from -6 to 6
- key_cache: bfloat16 [256, 128, 3072], P('req', None, 'tp'), may hold values from -420 to 420
- value_cache: bfloat16 [256, 128, 3072], P('req', None, 'tp'), may hold values from -6 to 6
- slot_owner: int32 [256], P('req'), may hold values from -1 to 255, as said below
- slot_page: int32 [256], P('req'), may hold values from 0 to 127, as said below
- cache_lengths: int32 [256], replicated, may hold values from 0 to 16384, as said below
- span_offsets: int32 [32], replicated, may hold values from 0 to 4096
Outputs:
- new_hidden: bfloat16 [9472, 5120], P('req', 'tp')
Inputs may be any that keep to these rules, and one draw needn't show every extreme that they name: Each pool slot holds one page of decode request slot_owner[s], or nothing where it is -1. No page of a request is held twice, and a request holding c pages holds pages 0 to c - 1. `slot_page`: 0 for a slot that holds nothing. `cache_lengths`: A request holding c pages of the pool has a length from (c - 1) * 128 + 1 to c * 128, and 0 where c = 0.
All inputs are finite; a program needn't handle non-finite values.
Results may differ from a plain program's by a relative error of at most 0.0076.
Values may be sent and summed in bfloat16 or wider, within the bound.
A program may use at most 128 MiB of HBM per device.

v0:
```python
import jax
import jax.numpy as jnp
from jax import lax
from jax.sharding import PartitionSpec as P

HD = 128
SPAN = 288
DEC = 8
EPSILON = 1e-06
THETA = 500000.0
NEGATIVE = -1e30


def rotate(values, positions):
    half_width = values.shape[-1] // 2
    frequency = THETA ** (-(jnp.arange(half_width, dtype=jnp.float32) * 2.0 / values.shape[-1]))
    angles = positions.astype(jnp.float32)[:, None] * frequency[None, :]
    cosine = jnp.cos(angles)[:, None, :]
    sine_part = jnp.sin(angles)[:, None, :]
    first_half = values[..., :half_width]
    second = values[..., half_width:]
    return jnp.concatenate(
        [first_half * cosine - second * sine_part, second * cosine + first_half * sine_part], -1
    )


def softmax_part(scores, key_mask, values, form):
    masked = jnp.where(key_mask, scores, NEGATIVE)
    top_score = jnp.max(masked, -1)
    exp_terms = jnp.where(key_mask, jnp.exp(masked - top_score[..., None]), 0.0)
    weight_sum = jnp.sum(exp_terms, -1)
    numerator = jnp.einsum(
        form, exp_terms.astype(jnp.bfloat16), values, preferred_element_type=jnp.float32
    )
    return (top_score, weight_sum, numerator)


def merge_parts(top_scores, weight_sums, numerators):
    best_score = jnp.max(top_scores, 0)
    factor = jnp.exp(top_scores - best_score[None])
    weight_sum = jnp.sum(factor * weight_sums, 0)
    numerator = jnp.sum(factor[..., None] * numerators, 0)
    return numerator / weight_sum[..., None]


def body(
    hidden,
    raw_q,
    raw_k,
    raw_v,
    q_gain,
    k_gain,
    out_weight,
    post_gain,
    prefix_keys,
    prefix_values,
    key_cache,
    value_cache,
    slot_owner,
    slot_page,
    cache_lengths,
    span_offsets,
):
    groups = lax.axis_size("req")
    my_group = lax.axis_index("req")
    tp_count = lax.axis_size("tp")
    rows_group = SPAN + DEC
    local_width = raw_q.shape[1]
    local_heads = local_width // HD
    requests = groups * DEC
    score_scale = HD ** (-0.5)
    page_rows = key_cache.shape[1]
    own_keys = lax.all_to_all(prefix_keys, "req", split_axis=0, concat_axis=1, tiled=True)
    own_values = lax.all_to_all(prefix_values, "req", split_axis=0, concat_axis=1, tiled=True)
    prefix_len = own_keys.shape[1] * page_rows
    own_keys = own_keys.reshape(prefix_len, local_heads, HD)
    own_values = own_values.reshape(prefix_len, local_heads, HD)
    own_lengths = lax.dynamic_slice_in_dim(cache_lengths, my_group * DEC, DEC)
    positions = jnp.concatenate(
        [span_offsets[my_group] + jnp.arange(SPAN, dtype=jnp.int32), own_lengths]
    )
    float_query = raw_q.astype(jnp.float32)
    float_key = raw_k.astype(jnp.float32)
    query_power, key_power = lax.psum(
        (jnp.sum(float_query * float_query, 1), jnp.sum(float_key * float_key, 1)), "tp"
    )
    full_width = local_width * tp_count
    normed_query = (
        float_query * lax.rsqrt(query_power / full_width + EPSILON)[:, None] * q_gain[None, :]
    )
    normed_key = float_key * lax.rsqrt(key_power / full_width + EPSILON)[:, None] * k_gain[None, :]
    query = rotate(normed_query.reshape(rows_group, local_heads, HD), positions).astype(
        jnp.bfloat16
    )
    key_rows = rotate(normed_key.reshape(rows_group, local_heads, HD), positions).astype(
        jnp.bfloat16
    )
    value_rows = raw_v.reshape(rows_group, local_heads, HD)
    decode_queries = lax.all_gather(query[SPAN:], "req", axis=0, tiled=True)
    live_slot = slot_owner >= 0
    owner_index = jnp.maximum(slot_owner, 0)
    slot_queries = decode_queries[owner_index]
    slot_keys = key_cache.reshape(key_cache.shape[0], page_rows, local_heads, HD)
    slot_values = value_cache.reshape(value_cache.shape[0], page_rows, local_heads, HD)
    scores = (
        jnp.einsum("shd,sphd->shp", slot_queries, slot_keys, preferred_element_type=jnp.float32)
        * score_scale
    )
    key_pos = slot_page[:, None] * page_rows + jnp.arange(page_rows, dtype=jnp.int32)[None, :]
    key_mask = live_slot[:, None] & (key_pos < cache_lengths[owner_index][:, None])
    top_score, weight_sum, numerator = softmax_part(
        scores, key_mask[:, None, :], slot_values, "shp,sphd->shd"
    )
    member = slot_owner[None, :] == jnp.arange(requests, dtype=jnp.int32)[:, None]
    best_score = jnp.max(jnp.where(member[:, :, None], top_score[None], NEGATIVE), 1)
    factor = jnp.where(member[:, :, None], jnp.exp(top_score[None] - best_score[:, None]), 0.0)
    request_total = jnp.einsum("rsh,sh->rh", factor, weight_sum, precision=lax.Precision.HIGHEST)
    request_numerator = jnp.einsum(
        "rsh,shd->rhd", factor, numerator, precision=lax.Precision.HIGHEST
    )
    packed = jnp.concatenate(
        [request_numerator, best_score[..., None], request_total[..., None]], -1
    )
    back = lax.all_to_all(packed, "req", split_axis=0, concat_axis=0, tiled=True)
    back = back.reshape(groups, DEC, local_heads, HD + 2)
    own_scores = (
        jnp.sum(query[SPAN:].astype(jnp.float32) * key_rows[SPAN:].astype(jnp.float32), -1)
        * score_scale
    )
    decode_out = merge_parts(
        jnp.concatenate([back[..., HD], own_scores[None]], 0),
        jnp.concatenate([back[..., HD + 1], jnp.ones_like(own_scores)[None]], 0),
        jnp.concatenate([back[..., :HD], value_rows[SPAN:].astype(jnp.float32)[None]], 0),
    )
    span_query = query[:SPAN]
    causal = jnp.arange(SPAN)[:, None] >= jnp.arange(SPAN)[None, :]
    prefix_mask = jnp.arange(prefix_len, dtype=jnp.int32) < span_offsets[my_group]
    pre_scores = (
        jnp.einsum("qhd,khd->qhk", span_query, own_keys, preferred_element_type=jnp.float32)
        * score_scale
    )
    self_scores = (
        jnp.einsum("qhd,khd->qhk", span_query, key_rows[:SPAN], preferred_element_type=jnp.float32)
        * score_scale
    )
    pre_masked = jnp.where(prefix_mask[None, None, :], pre_scores, NEGATIVE)
    self_masked = jnp.where(causal[:, None, :], self_scores, NEGATIVE)
    top = jnp.maximum(jnp.max(pre_masked, -1), jnp.max(self_masked, -1))
    pre_exp = jnp.where(prefix_mask[None, None, :], jnp.exp(pre_masked - top[..., None]), 0.0)
    self_exp = jnp.where(causal[:, None, :], jnp.exp(self_masked - top[..., None]), 0.0)
    total = jnp.sum(pre_exp, -1) + jnp.sum(self_exp, -1)
    span_numerator = jnp.einsum(
        "qhk,khd->qhd", pre_exp.astype(jnp.bfloat16), own_values, preferred_element_type=jnp.float32
    ) + jnp.einsum(
        "qhk,khd->qhd",
        self_exp.astype(jnp.bfloat16),
        value_rows[:SPAN],
        preferred_element_type=jnp.float32,
    )
    span_out = span_numerator / total[..., None]
    merged = jnp.concatenate([span_out, decode_out], 0)
    attention = merged.reshape(rows_group, local_width).astype(jnp.bfloat16)
    share_width = post_gain.shape[0]
    partial = jnp.dot(attention, out_weight, preferred_element_type=jnp.float32)
    my_share = lax.psum_scatter(partial, "tp", scatter_dimension=1, tiled=True)
    power = lax.psum(jnp.sum(my_share * my_share, 1), "tp")
    inverse = lax.rsqrt(power / (share_width * tp_count) + EPSILON)
    normed = my_share * inverse[:, None]
    return (hidden.astype(jnp.float32) + normed * post_gain[None, :]).astype(jnp.bfloat16)


def solution(mesh):
    return jax.shard_map(
        body,
        mesh=mesh,
        in_specs=(
            P("req", "tp"),
            P("req", "tp"),
            P("req", "tp"),
            P("req", "tp"),
            P("tp"),
            P("tp"),
            P("tp", None),
            P("tp"),
            P(None, "req", None, "tp"),
            P(None, "req", None, "tp"),
            P("req", None, "tp"),
            P("req", None, "tp"),
            P("req"),
            P("req"),
            P(),
            P(),
        ),
        out_specs=P("req", "tp"),
        check_vma=False,
    )
```

profile of v0, /device:TPU:8, one launch (start us, length us, event | category | flops | bytes accessed | tf_op | source)
XLA Modules:
  0.0 327.7 jit_solution(14584163546658143109)
XLA Ops:
  8.6 1.6 copy.111
  10.2 1.1 fusion.22
  11.3 1.1 fusion.24
  12.4 14.6 %all-reduce.1 = (f32[296]{0:T(512)S(1)}, f32[296]{0:T(512)S(1)}) all-reduce(f32[296]{0:T(512)S(1)} %fusion.22, f32[296]{0:T(512)S(1)} %fusion.24), channel_id=1, replica_groups=mesh['req'=32,'tp'=8] {'tp'}, use_global_device_ids=true, to_apply=%region_1.0 | all-reduce | flops 592 | bytes 4736 | tf_op jit(solution)/shard_map/psum | solution.py:84
  30.3 1.2 fusion.70
  32.3 1.3 subtract_convert_fusion.1
  34.5 52.2 %all_gather.3 = bf16[256,3,128]{2,0,1:T(8,128)(2,1)S(1)} all-gather(bf16[8,3,128]{2,0,1:T(8,128)(2,1)S(1)} %get-tuple-element.10), channel_id=1, replica_groups=mesh['req'=32,'tp'=8] {'req'}, dimensions={0}, use_global_device_ids=true | all-gather | bytes 202752 | tf_op jit(solution)/shard_map/all_gather | solution.py:99
  89.1 1.5 copy.112
  92.1 1.3 reshape.274
  93.5 21.6 %all_to_all.23 = f32[32,1,3120]{2,1,0:T(1,128)} all-to-all(f32[32,1,3120]{2,1,0:T(1,128)S(1)} %reshape.274), channel_id=1, replica_groups=mesh['req'=32,'tp'=8] {'req'}, dimensions={0} | all-to-all | bytes 798720 | tf_op jit(solution)/shard_map/all_to_all | solution.py:124
  115.1 67.9 %all_to_all.24 = bf16[32,1,128,384]{3,2,1,0:T(8,128)(2,1)} all-to-all(bf16[32,1,128,384]{3,2,1,0:T(8,128)(2,1)} %param.24), channel_id=1, replica_groups=mesh['req'=32,'tp'=8] {'req'}, dimensions={0} | all-to-all | bytes 6291456 | tf_op jit(solution)/shard_map/all_to_all | solution.py:73
  183.0 8.2 %all-to-all-start.1 = ((bf16[32,1,128,384]{3,2,1,0:T(8,128)(2,1)}), bf16[32,1,128,384]{3,2,1,0:T(8,128)(2,1)S(1)}, u32[]{:S(2)}, u32[]{:S(2)}) async-start(bf16[32,1,128,384]{3,2,1,0:T(8,128)(2,1)} %param.25), calls=%async_computation.1 | async-start | bytes 6291456 | tf_op jit(solution)/shard_map/all_to_all | solution.py:74
  191.9 1.3 bitcast_convert_fusion
  193.2 3.3 %fusion.71 = (f32[288,3]{0,1:T(4,128)}, f32[288,3,288]{0,2,1:T(8,128)}) fusion(bf16[296,3,64]{2,0,1:T(8,128)(2,1)S(1)} %get-tuple-element.11, bf16[296,3,64]{2,0,1:T(8,128)(2,1)} %copy-done.2, bf16[296,3,64]{2,0,1:T(8,128)(2,1)} %copy-done.5, bf16[296,3,64]{2,0,1:T(8,128)(2,1)} %copy-done.4, pred[288,288]{0,1:T(8,128)(4,1)S(1)} %iota_compare_fusion), kind=kOutput, calls=%fused_computation.124 | convolution fusion | flops 65331360 | bytes 1536384 | tf_op jit(solution)/shard_map/qhd,khd->qhk/dot_general | solution.py:143
  197.0 3.3 %reduce.3 = f32[32,3120]{1,0:T(8,128)} reduce(f32[32,1,3120]{2,1,0:T(1,128)} %all_to_all.23, f32[]{:T(128)} %broadcast.170), dimensions={1}, to_apply=%all_to_all.8.reduce_sub_computation | reduce | bytes 798724 | tf_op jit(solution)/shard_map/all_to_all | solution.py:124
  200.3 3.3 %reshape.275 = f32[256,3,130]{2,1,0:T(4,128)} reshape(f32[32,3120]{1,0:T(8,128)} %reduce.3) | data formatting | bytes 798720
  203.6 1.4 copy.184
  206.8 1.2 copy.118
  208.1 1.2 copy.115
  210.8 1.2 fusion.26
  212.1 9.2 %reshape.272 = bf16[4096,3,128]{2,1,0:T(4,128)(2,1)} reshape(bf16[32,1,128,384]{3,2,1,0:T(8,128)(2,1)} %all_to_all.24) | data formatting | bytes 6291456 | tf_op jit(solution)/shard_map/reshape | solution.py:76
  221.3 9.9 %bitcast_reduce_fusion = (f32[288,3]{0,1:T(4,128)S(1)}, f32[3,288,4096]{2,1,0:T(8,128)}) fusion(pred[4096]{0:T(1024)(128)(4,1)S(1)} %iota_compare_fusion.1, bf16[4096,3,128]{2,1,0:T(4,128)(2,1)} %reshape.272, bf16[296,3,64]{2,0,1:T(8,128)(2,1)S(1)} %get-tuple-element.11, bf16[296,3,64]{2,0,1:T(8,128)(2,1)} %copy-done.2), kind=kOutput, calls=%fused_computation.3 | convolution fusion | flops 917027968 | bytes 17536384 | tf_op jit(solution)/shard_map/qhd,khd->qhk/dot_general | solution.py:139
  231.2 8.9 %fusion.2 = f32[288,3]{0,1:T(4,128)S(1)} fusion(f32[3,288,4096]{2,1,0:T(8,128)} %get-tuple-element.31, f32[288,3]{0,1:T(4,128)S(1)} %max.10, pred[4096]{0:T(1024)(128)(4,1)S(1)} %iota_compare_fusion.1), kind=kLoop, calls=%fused_computation.7 | loop fusion | flops 17693856 | bytes 14166784 | tf_op jit(solution)/shard_map/reduce_sum | solution.py:151
  240.1 6.7 %all-to-all-done.1 = bf16[32,1,128,384]{3,2,1,0:T(8,128)(2,1)S(1)} async-done(((bf16[32,1,128,384]{3,2,1,0:T(8,128)(2,1)}), bf16[32,1,128,384]{3,2,1,0:T(8,128)(2,1)S(1)}, u32[]{:S(2)}, u32[]{:S(2)}) %all-to-all-start.1) | async-done | bytes 3145760 | tf_op jit(solution)/shard_map/all_to_all | solution.py:74
  246.8 3.9 %reshape.273 = bf16[4096,3,128]{2,1,0:T(4,128)(2,1)} reshape(bf16[32,1,128,384]{3,2,1,0:T(8,128)(2,1)S(1)} %all-to-all-done.1) | data formatting | bytes 6291456 | tf_op jit(solution)/shard_map/reshape | solution.py:77
  250.6 8.6 %fusion.4 = f32[3,288,128]{2,1,0:T(8,128)S(1)} fusion(f32[3,288,4096]{2,1,0:T(8,128)} %get-tuple-element.31, f32[288,3]{0,1:T(4,128)S(1)} %max.10, pred[4096]{0:T(1024)(128)(4,1)S(1)} %iota_compare_fusion.1, bf16[4096,3,128]{2,1,0:T(4,128)(2,1)} %reshape.273), kind=kOutput, calls=%fused_computation.9 | convolution fusion | flops 923664384 | bytes 17751424 | tf_op jit(solution)/shard_map/qhk,khd->qhd/dot_general | solution.py:152
  260.1 1.3 copy-done.1
  261.3 4.4 %fusion.27 = f32[296,5120]{1,0:T(8,128)} fusion(bf16[384,5120]{1,0:T(8,128)(2,1)S(1)} %copy-done.1, bf16[8,3,128]{2,0,1:T(8,128)(2,1)S(1)} %divide_convert_fusion, bf16[288,3,128]{2,0,1:T(8,128)(2,1)S(1)} %fusion.15), kind=kOutput, calls=%fused_computation.48 | convolution fusion | flops 1164374016 | bytes 10221568 | tf_op jit(solution)/shard_map/dot_general | solution.py:164
  265.7 37.9 %reduce-scatter.2.cloned.1.call-done = f32[296,640]{1,0:T(8,128)} async-done(((f32[296,5120]{1,0:T(8,128)}), f32[296,640]{1,0:T(8,128)}) %reduce-scatter.2.cloned.1.call-update) | async-done | bytes 757776 | tf_op jit(solution)/shard_map/reduce_scatter | solution.py:165
  303.6 1.3 multiply_reduce_fusion
  304.9 13.9 %psum.23 = f32[296]{0:T(512)S(1)} all-reduce(f32[296]{0:T(512)S(1)} %multiply_reduce_fusion), channel_id=1, replica_groups=mesh['req'=32,'tp'=8] {'tp'}, use_global_device_ids=true, to_apply=%region_17.18 | all-reduce | flops 296 | bytes 2368 | tf_op jit(solution)/shard_map/psum | solution.py:166
  318.8 2.1 add_convert_fusion
  (78 shorter events, 16.3 us)
Async XLA Ops:
  6.5 23.4 %copy-start.6 = (bf16[296,384]{1,0:T(8,128)(2,1)S(1)}, bf16[296,384]{1,0:T(8,128)(2,1)}, u32[]{:S(2)}) copy-start(bf16[296,384]{1,0:T(8,128)(2,1)} %param.18) | copy-start | bytes 681988
  6.5 22.2 %copy-start.12 = (s32[32]{0:T(128)S(1)}, s32[32]{0:T(128)}, u32[]{:S(2)}) copy-start(s32[32]{0:T(128)} %param.31) | copy-start | bytes 388
  6.5 23.5 %copy-start.10 = (f32[384]{0:T(512)S(1)}, f32[384]{0:T(512)}, u32[]{:S(2)}) copy-start(f32[384]{0:T(512)} %param.21) | copy-start | bytes 4612
  12.4 19.1 %copy-start = (s32[256]{0:T(256)S(1)}, s32[256]{0:T(256)}, u32[]{:S(2)}) copy-start(s32[256]{0:T(256)} %param.30) | copy-start | bytes 3076
  30.3 57.8 %copy-start.13 = (s32[8]{0:T(128)S(1)}, s32[8]{0:T(128)}, u32[]{:S(2)}) copy-start(s32[8]{0:T(128)} %param.29) | copy-start | bytes 100
  33.6 0.7 copy-start.5
  33.6 55.5 %copy-start.2 = (bf16[296,3,64]{2,0,1:T(8,128)(2,1)}, bf16[296,3,64]{2,0,1:T(8,128)(2,1)S(1)}, u32[]{:S(2)}) copy-start(bf16[296,3,64]{2,0,1:T(8,128)(2,1)S(1)} %get-tuple-element.12) | copy-start | bytes 340996
  33.6 55.5 %copy-start.4 = (bf16[296,3,64]{2,0,1:T(8,128)(2,1)}, bf16[296,3,64]{2,0,1:T(8,128)(2,1)S(1)}, u32[]{:S(2)}) copy-start(bf16[296,3,64]{2,0,1:T(8,128)(2,1)S(1)} %get-tuple-element.22) | copy-start | bytes 340996
  183.0 63.8 %all-to-all-start.1 = ((bf16[32,1,128,384]{3,2,1,0:T(8,128)(2,1)}), bf16[32,1,128,384]{3,2,1,0:T(8,128)(2,1)S(1)}, u32[]{:S(2)}, u32[]{:S(2)}) async-start(bf16[32,1,128,384]{3,2,1,0:T(8,128)(2,1)} %param.25), calls=%async_computation.1 | async-start | bytes 6291456 | tf_op jit(solution)/shard_map/all_to_all | solution.py:74
  191.2 112.4 %reduce-scatter.2.cloned.1.call-start = ((), (), s32[]{:S(2)}) async-start(), calls=%async_computation.4 | async-start | bytes 6819840 | tf_op jit(solution)/shard_map/reduce_scatter | solution.py:165
  221.3 9.9 %copy-start.8 = (f32[288,3]{0,1:T(4,128)S(1)}, f32[288,3]{0,1:T(4,128)}, u32[]{:S(2)}) copy-start(f32[288,3]{0,1:T(4,128)} %get-tuple-element.32) | copy-start | bytes 10372
  250.6 8.6 %copy-start.3 = (f32[288,3,288]{0,2,1:T(8,128)S(1)}, f32[288,3,288]{0,2,1:T(8,128)}, u32[]{:S(2)}) copy-start(f32[288,3,288]{0,2,1:T(8,128)} %get-tuple-element.33) | copy-start | bytes 2985988
  250.6 8.9 %copy-start.11 = (bf16[296,384]{1,0:T(8,128)(2,1)S(1)}, bf16[296,384]{1,0:T(8,128)(2,1)}, u32[]{:S(2)}) copy-start(bf16[296,384]{1,0:T(8,128)(2,1)} %param.19) | copy-start | bytes 681988
  259.2 2.1 copy-start.1
  265.7 53.1 %copy-start.7 = (bf16[296,640]{1,0:T(8,128)(2,1)S(1)}, bf16[296,640]{1,0:T(8,128)(2,1)}, u32[]{:S(2)}) copy-start(bf16[296,640]{1,0:T(8,128)(2,1)} %param.16) | copy-start | bytes 1136644
  265.7 53.1 %copy-start.9 = (f32[640]{0:T(1024)S(1)}, f32[640]{0:T(1024)}, u32[]{:S(2)}) copy-start(f32[640]{0:T(1024)} %param.23) | copy-start | bytes 7684
Sparse Core Ops, SparseCore 0:
  265.8 37.7 reduce-scatter.1
where the time goes:
time: 329 us; the launch traced here: 328 us
  blocking collectives  170 us (52%)
  waiting for transfers between devices  44.6 us (14%)
  local copies, waits for them, and re-layouts  33.2 us (10%)
  other arithmetic  29.4 us (9%)
  matrix products  28.3 us (9%)
  between operations  13.7 us (4%)
  starting transfers between devices  8.25 us (3%)
    all_to_all x1, blocking collectives, body(): lax.all_to_all(prefix_keys, 'req', split_axis=0, concat_axis=1, tiled=True)  67.9 us
    all_gather x1, blocking collectives, body(): decode_queries = lax.all_gather(query[SPAN:], 'req', axis=0, tiled=True)  52.2 us
    reduce_scatter x1, waiting for transfers between devices, body(): my_share = lax.psum_scatter(partial, 'tp', scatter_dimension=1, tiled=True)  37.9 us
    all_to_all x1, blocking collectives, body(): lax.all_to_all(packed, 'req', split_axis=0, concat_axis=0, tiled=True)  21.6 us
    psum x1, blocking collectives, body(): lax.psum((jnp.sum(float_query * float_query, 1), jnp.sum(float_key * floa...  14.6 us
    psum x1, blocking collectives, body(): power = lax.psum(jnp.sum(my_share * my_share, 1), 'tp')  13.9 us
    dot_general x1, matrix products, body(): jnp.einsum('qhd,khd->qhk', span_query, own_keys, preferred_element_type=j...  9.93 us
    unnamed x32, local copies, waits for them, and re-layouts  9.72 us
  transfers between devices with their start and end apart: 2, of which 2 were waited for; matrix products, arithmetic and copies ran while one was open for 15% of the time, Pallas kernels for 0%

commit v1 on v0

--- a/solution.py
+++ b/solution.py
@@ -9,6 +9,13 @@
 EPSILON = 1e-06
 THETA = 500000.0
 NEGATIVE = -1e30
+
+
+def swapped_in(array, mesh_axis, d):
+    size = lax.axis_size(mesh_axis)
+    blocks = jnp.stack([array for _ in range(size)])
+    blocks = lax.all_to_all(blocks, mesh_axis, split_axis=0, concat_axis=0)
+    return jnp.concatenate(blocks, axis=d)
 
 
 def rotate(values, positions):
@@ -96,7 +103,7 @@
         jnp.bfloat16
     )
     value_rows = raw_v.reshape(rows_group, local_heads, HD)
-    decode_queries = lax.all_gather(query[SPAN:], "req", axis=0, tiled=True)
+    decode_queries = swapped_in(query[SPAN:], "req", 0)
     live_slot = slot_owner >= 0
     owner_index = jnp.maximum(slot_owner, 0)
     slot_queries = decode_queries[owner_index]

time: 329 us -> 313 us (0.951)
  blocking collectives: 170 us -> 120 us
  waiting for transfers between devices: 44.6 us -> 72.6 us
  starting transfers between devices: 8.25 us -> 17.3 us
    all_gather x1 -> x0, blocking collectives: 52.2 us -> none  [body(): decode_queries = lax.all_gather(query[SPAN:], 'req', axis=0, tiled=True)]
    all_to_all x1, waiting for transfers between devices: 6.65 us -> 19.1 us  [body(): lax.all_to_all(prefix_values, 'req', split_axis=0, concat_axis=1, tiled=T...]
    all_to_all x0 -> x1, starting transfers between devices: none -> 11.7 us  [swapped_in(): blocks = lax.all_to_all(blocks, mesh_axis, split_axis=0, concat_axis=0)]
    reduce_scatter x1, waiting for transfers between devices: 37.9 us -> 48.1 us  [body(): my_share = lax.psum_scatter(partial, 'tp', scatter_dimension=1, tiled=True)]
    all_to_all x1, blocking collectives: 67.9 us -> 75 us  [body(): lax.all_to_all(prefix_keys, 'req', split_axis=0, concat_axis=1, tiled=True)]
    all_to_all x0 -> x1, waiting for transfers between devices: none -> 5.31 us  [swapped_in(): blocks = lax.all_to_all(blocks, mesh_axis, split_axis=0, concat_axis=0)]
    all_to_all x1, blocking collectives: 21.6 us -> 16.8 us  [body(): lax.all_to_all(packed, 'req', split_axis=0, concat_axis=0, tiled=True)]
    unnamed x32 -> x34, local copies, waits for them, and re-layouts: 9.72 us -> 9.65 us
  transfers between devices with their start and end apart: 2 -> 3, of which waited for: 2 -> 3; matrix products, arithmetic and copies ran while one was open for 15% -> 17% of each run, Pallas kernels for 0% -> 0%
where the time goes in v1:
time: 313 us; the launch traced here: 312 us
  blocking collectives  120 us (38%)
  waiting for transfers between devices  72.6 us (23%)
  local copies, waits for them, and re-layouts  33.1 us (11%)
  matrix products  28.3 us (9%)
  other arithmetic  26.4 us (8%)
  starting transfers between devices  17.3 us (6%)
  between operations  13.8 us (4%)
    all_to_all x1, blocking collectives, body(): lax.all_to_all(prefix_keys, 'req', split_axis=0, concat_axis=1, tiled=True)  75 us
    reduce_scatter x1, waiting for transfers between devices, body(): my_share = lax.psum_scatter(partial, 'tp', scatter_dimension=1, tiled=True)  48.1 us
    all_to_all x1, waiting for transfers between devices, body(): lax.all_to_all(prefix_values, 'req', split_axis=0, concat_axis=1, tiled=T...  19.1 us
    all_to_all x1, blocking collectives, body(): lax.all_to_all(packed, 'req', split_axis=0, concat_axis=0, tiled=True)  16.8 us
    psum x1, blocking collectives, body(): lax.psum((jnp.sum(float_query * float_query, 1), jnp.sum(float_key * floa...  14.6 us
    psum x1, blocking collectives, body(): power = lax.psum(jnp.sum(my_share * my_share, 1), 'tp')  13.9 us
    all_to_all x1, starting transfers between devices, swapped_in(): blocks = lax.all_to_all(blocks, mesh_axis, split_axis=0, concat_axis=0)  11.7 us
    dot_general x1, matrix products, body(): jnp.einsum('qhd,khd->qhk', span_query, own_keys, preferred_element_type=j...  9.93 us
  transfers between devices with their start and end apart: 3, of which 3 were waited for; matrix products, arithmetic and copies ran while one was open for 17% of the time, Pallas kernels for 0%

profile of v1, /device:TPU:8, one launch (start us, length us, event | category | flops | bytes accessed | tf_op | source)
XLA Modules:
  0.0 311.8 jit_solution(12591946263039529448)
XLA Ops:
  6.6 1.1 fusion.22
  7.7 1.1 fusion.24
  8.8 14.6 %all-reduce.1 = (f32[296]{0:T(512)S(1)}, f32[296]{0:T(512)S(1)}) all-reduce(f32[296]{0:T(512)S(1)} %fusion.22, f32[296]{0:T(512)S(1)} %fusion.24), channel_id=1, replica_groups=mesh['req'=32,'tp'=8] {'tp'}, use_global_device_ids=true, to_apply=%region_1.0 | all-reduce | flops 592 | bytes 4736 | tf_op jit(solution)/shard_map/psum | solution.py:91
  23.4 1.1 fusion.23
  29.7 11.7 %all-to-all-start.2 = ((bf16[32,8,3,128]{3,1,2,0:T(8,128)(2,1)}), bf16[32,8,3,128]{3,1,2,0:T(8,128)(2,1)S(1)}, u32[]{:S(2)}, u32[]{:S(2)}) async-start(bf16[32,8,3,128]{3,1,2,0:T(8,128)(2,1)} %stack.2), calls=%async_computation.2 | async-start | bytes 393216 | tf_op jit(solution)/shard_map/all_to_all | solution.py:17
  41.5 1.5 copy.155
  43.7 1.5 copy.156
  45.3 5.3 %all-to-all-done.2 = bf16[32,8,3,128]{3,1,2,0:T(8,128)(2,1)S(1)} async-done(((bf16[32,8,3,128]{3,1,2,0:T(8,128)(2,1)}), bf16[32,8,3,128]{3,1,2,0:T(8,128)(2,1)S(1)}, u32[]{:S(2)}, u32[]{:S(2)}) %all-to-all-start.2) | async-done | bytes 196640 | tf_op jit(solution)/shard_map/all_to_all | solution.py:17
  53.9 1.3 reshape.280
  55.2 16.8 %all_to_all.28 = f32[32,1,3120]{2,1,0:T(1,128)} all-to-all(f32[32,1,3120]{2,1,0:T(1,128)S(1)} %reshape.280), channel_id=1, replica_groups=mesh['req'=32,'tp'=8] {'req'}, dimensions={0} | all-to-all | bytes 798720 | tf_op jit(solution)/shard_map/all_to_all | solution.py:131
  72.0 75.0 %all_to_all.29 = bf16[32,1,128,384]{3,2,1,0:T(8,128)(2,1)} all-to-all(bf16[32,1,128,384]{3,2,1,0:T(8,128)(2,1)} %param.24), channel_id=1, replica_groups=mesh['req'=32,'tp'=8] {'req'}, dimensions={0} | all-to-all | bytes 6291456 | tf_op jit(solution)/shard_map/all_to_all | solution.py:80
  147.0 5.6 %all-to-all-start.1 = ((bf16[32,1,128,384]{3,2,1,0:T(8,128)(2,1)}), bf16[32,1,128,384]{3,2,1,0:T(8,128)(2,1)S(1)}, u32[]{:S(2)}, u32[]{:S(2)}) async-start(bf16[32,1,128,384]{3,2,1,0:T(8,128)(2,1)} %param.25), calls=%async_computation.1 | async-start | bytes 6291456 | tf_op jit(solution)/shard_map/all_to_all | solution.py:81
  153.3 1.3 bitcast_convert_fusion
  154.6 3.3 %fusion.71 = (f32[288,3]{0,1:T(4,128)}, f32[288,3,288]{0,2,1:T(8,128)}) fusion(bf16[296,3,64]{2,0,1:T(8,128)(2,1)S(1)} %get-tuple-element.11, bf16[296,3,64]{2,0,1:T(8,128)(2,1)} %copy-done.2, bf16[296,3,64]{2,0,1:T(8,128)(2,1)} %copy-done.5, bf16[296,3,64]{2,0,1:T(8,128)(2,1)} %copy-done.4, pred[288,288]{0,1:T(8,128)(4,1)S(1)} %iota_compare_fusion), kind=kOutput, calls=%fused_computation.125 | convolution fusion | flops 65331360 | bytes 1536384 | tf_op jit(solution)/shard_map/qhd,khd->qhk/dot_general | solution.py:150
  158.4 3.3 %reduce.3 = f32[32,3120]{1,0:T(8,128)} reduce(f32[32,1,3120]{2,1,0:T(1,128)} %all_to_all.28, f32[]{:T(128)} %broadcast.172), dimensions={1}, to_apply=%all_to_all.11.reduce_sub_computation | reduce | bytes 798724 | tf_op jit(solution)/shard_map/all_to_all | solution.py:131
  161.7 3.3 %reshape.281 = f32[256,3,130]{2,1,0:T(4,128)} reshape(f32[32,3120]{1,0:T(8,128)} %reduce.3) | data formatting | bytes 798720
  165.0 1.4 copy.229
  168.2 1.2 copy.162
  169.5 1.2 copy.159
  172.2 1.2 fusion.26
  173.5 9.2 %reshape.278 = bf16[4096,3,128]{2,1,0:T(4,128)(2,1)} reshape(bf16[32,1,128,384]{3,2,1,0:T(8,128)(2,1)} %all_to_all.29) | data formatting | bytes 6291456 | tf_op jit(solution)/shard_map/reshape | solution.py:83
  182.7 9.9 %bitcast_reduce_fusion = (f32[288,3]{0,1:T(4,128)S(1)}, f32[3,288,4096]{2,1,0:T(8,128)}) fusion(pred[4096]{0:T(1024)(128)(4,1)S(1)} %iota_compare_fusion.1, bf16[4096,3,128]{2,1,0:T(4,128)(2,1)} %reshape.278, bf16[296,3,64]{2,0,1:T(8,128)(2,1)S(1)} %get-tuple-element.11, bf16[296,3,64]{2,0,1:T(8,128)(2,1)} %copy-done.2), kind=kOutput, calls=%fused_computation.3 | convolution fusion | flops 917027968 | bytes 17536384 | tf_op jit(solution)/shard_map/qhd,khd->qhk/dot_general | solution.py:146
  192.6 8.9 %fusion.2 = f32[288,3]{0,1:T(4,128)S(1)} fusion(f32[3,288,4096]{2,1,0:T(8,128)} %get-tuple-element.31, f32[288,3]{0,1:T(4,128)S(1)} %max.10, pred[4096]{0:T(1024)(128)(4,1)S(1)} %iota_compare_fusion.1), kind=kLoop, calls=%fused_computation.7 | loop fusion | flops 17693856 | bytes 14166784 | tf_op jit(solution)/shard_map/reduce_sum | solution.py:158
  201.5 19.1 %all-to-all-done.1 = bf16[32,1,128,384]{3,2,1,0:T(8,128)(2,1)S(1)} async-done(((bf16[32,1,128,384]{3,2,1,0:T(8,128)(2,1)}), bf16[32,1,128,384]{3,2,1,0:T(8,128)(2,1)S(1)}, u32[]{:S(2)}, u32[]{:S(2)}) %all-to-all-start.1) | async-done | bytes 3145760 | tf_op jit(solution)/shard_map/all_to_all | solution.py:81
  220.6 3.9 %reshape.279 = bf16[4096,3,128]{2,1,0:T(4,128)(2,1)} reshape(bf16[32,1,128,384]{3,2,1,0:T(8,128)(2,1)S(1)} %all-to-all-done.1) | data formatting | bytes 6291456 | tf_op jit(solution)/shard_map/reshape | solution.py:84
  224.5 8.6 %fusion.4 = f32[3,288,128]{2,1,0:T(8,128)S(1)} fusion(f32[3,288,4096]{2,1,0:T(8,128)} %get-tuple-element.31, f32[288,3]{0,1:T(4,128)S(1)} %max.10, pred[4096]{0:T(1024)(128)(4,1)S(1)} %iota_compare_fusion.1, bf16[4096,3,128]{2,1,0:T(4,128)(2,1)} %reshape.279), kind=kOutput, calls=%fused_computation.9 | convolution fusion | flops 923664384 | bytes 17751424 | tf_op jit(solution)/shard_map/qhk,khd->qhd/dot_general | solution.py:159
  233.9 1.3 copy-done.1
  235.2 4.4 %fusion.27 = f32[296,5120]{1,0:T(8,128)} fusion(bf16[384,5120]{1,0:T(8,128)(2,1)S(1)} %copy-done.1, bf16[8,3,128]{2,0,1:T(8,128)(2,1)S(1)} %divide_convert_fusion, bf16[288,3,128]{2,0,1:T(8,128)(2,1)S(1)} %fusion.15), kind=kOutput, calls=%fused_computation.48 | convolution fusion | flops 1164374016 | bytes 10221568 | tf_op jit(solution)/shard_map/dot_general | solution.py:171
  239.6 48.1 %reduce-scatter.2.cloned.1.call-done = f32[296,640]{1,0:T(8,128)} async-done(((f32[296,5120]{1,0:T(8,128)}), f32[296,640]{1,0:T(8,128)}) %reduce-scatter.2.cloned.1.call-update) | async-done | bytes 757776 | tf_op jit(solution)/shard_map/reduce_scatter | solution.py:172
  287.7 1.3 multiply_reduce_fusion
  289.0 13.9 %psum.23 = f32[296]{0:T(512)S(1)} all-reduce(f32[296]{0:T(512)S(1)} %multiply_reduce_fusion), channel_id=1, replica_groups=mesh['req'=32,'tp'=8] {'tp'}, use_global_device_ids=true, to_apply=%region_17.18 | all-reduce | flops 296 | bytes 2368 | tf_op jit(solution)/shard_map/psum | solution.py:173
  302.9 2.1 add_convert_fusion
  (83 shorter events, 14.6 us)
Async XLA Ops:
  6.5 19.8 %copy-start.6 = (bf16[296,384]{1,0:T(8,128)(2,1)S(1)}, bf16[296,384]{1,0:T(8,128)(2,1)}, u32[]{:S(2)}) copy-start(bf16[296,384]{1,0:T(8,128)(2,1)} %param.18) | copy-start | bytes 681988
  6.5 18.5 %copy-start.13 = (s32[32]{0:T(128)S(1)}, s32[32]{0:T(128)}, u32[]{:S(2)}) copy-start(s32[32]{0:T(128)} %param.31) | copy-start | bytes 388
  6.5 19.8 %copy-start.10 = (f32[384]{0:T(512)S(1)}, f32[384]{0:T(512)}, u32[]{:S(2)}) copy-start(f32[384]{0:T(512)} %param.21) | copy-start | bytes 4612
  8.8 18.3 %copy-start = (s32[256]{0:T(256)S(1)}, s32[256]{0:T(256)}, u32[]{:S(2)}) copy-start(s32[256]{0:T(256)} %param.30) | copy-start | bytes 3076
  26.7 14.7 %copy-start.11 = (s32[8]{0:T(128)S(1)}, s32[8]{0:T(128)}, u32[]{:S(2)}) copy-start(s32[8]{0:T(128)} %param.28) | copy-start | bytes 100
  27.9 17.3 %copy-start.14 = (s32[8]{0:T(128)S(1)}, s32[8]{0:T(128)}, u32[]{:S(2)}) copy-start(s32[8]{0:T(128)} %param.29) | copy-start | bytes 100
  28.1 0.7 copy-start.5
  28.1 14.9 %copy-start.2 = (bf16[296,3,64]{2,0,1:T(8,128)(2,1)}, bf16[296,3,64]{2,0,1:T(8,128)(2,1)S(1)}, u32[]{:S(2)}) copy-start(bf16[296,3,64]{2,0,1:T(8,128)(2,1)S(1)} %get-tuple-element.12) | copy-start | bytes 340996
  28.2 14.9 %copy-start.4 = (bf16[296,3,64]{2,0,1:T(8,128)(2,1)}, bf16[296,3,64]{2,0,1:T(8,128)(2,1)S(1)}, u32[]{:S(2)}) copy-start(bf16[296,3,64]{2,0,1:T(8,128)(2,1)S(1)} %get-tuple-element.22) | copy-start | bytes 340996
  29.7 20.9 %all-to-all-start.2 = ((bf16[32,8,3,128]{3,1,2,0:T(8,128)(2,1)}), bf16[32,8,3,128]{3,1,2,0:T(8,128)(2,1)S(1)}, u32[]{:S(2)}, u32[]{:S(2)}) async-start(bf16[32,8,3,128]{3,1,2,0:T(8,128)(2,1)} %stack.2), calls=%async_computation.2 | async-start | bytes 393216 | tf_op jit(solution)/shard_map/all_to_all | solution.py:17
  147.0 73.6 %all-to-all-start.1 = ((bf16[32,1,128,384]{3,2,1,0:T(8,128)(2,1)}), bf16[32,1,128,384]{3,2,1,0:T(8,128)(2,1)S(1)}, u32[]{:S(2)}, u32[]{:S(2)}) async-start(bf16[32,1,128,384]{3,2,1,0:T(8,128)(2,1)} %param.25), calls=%async_computation.1 | async-start | bytes 6291456 | tf_op jit(solution)/shard_map/all_to_all | solution.py:81
  152.6 135.1 %reduce-scatter.2.cloned.1.call-start = ((), (), s32[]{:S(2)}) async-start(), calls=%async_computation.5 | async-start | bytes 6819840 | tf_op jit(solution)/shard_map/reduce_scatter | solution.py:172
  182.7 9.9 %copy-start.8 = (f32[288,3]{0,1:T(4,128)S(1)}, f32[288,3]{0,1:T(4,128)}, u32[]{:S(2)}) copy-start(f32[288,3]{0,1:T(4,128)} %get-tuple-element.32) | copy-start | bytes 10372
  224.5 8.6 %copy-start.3 = (f32[288,3,288]{0,2,1:T(8,128)S(1)}, f32[288,3,288]{0,2,1:T(8,128)}, u32[]{:S(2)}) copy-start(f32[288,3,288]{0,2,1:T(8,128)} %get-tuple-element.33) | copy-start | bytes 2985988
  224.5 8.9 %copy-start.12 = (bf16[296,384]{1,0:T(8,128)(2,1)S(1)}, bf16[296,384]{1,0:T(8,128)(2,1)}, u32[]{:S(2)}) copy-start(bf16[296,384]{1,0:T(8,128)(2,1)} %param.19) | copy-start | bytes 681988
  233.0 2.1 copy-start.1
  239.5 63.3 %copy-start.7 = (bf16[296,640]{1,0:T(8,128)(2,1)S(1)}, bf16[296,640]{1,0:T(8,128)(2,1)}, u32[]{:S(2)}) copy-start(bf16[296,640]{1,0:T(8,128)(2,1)} %param.16) | copy-start | bytes 1136644
  239.5 63.4 %copy-start.9 = (f32[640]{0:T(1024)S(1)}, f32[640]{0:T(1024)}, u32[]{:S(2)}) copy-start(f32[640]{0:T(1024)} %param.23) | copy-start | bytes 7684
Sparse Core Ops, SparseCore 0:
  239.7 47.9 reduce-scatter.1
